TPU v7x, 32 devices: a whole 2x2x4 slice. The times are simulated.
32 devices in a mesh: dp: 8 (over y, x, core), seq: 4 (over z).
Axes of the slice: x: 2, y: 2, z: 4, core: 2. Of those that a mesh axis runs over, the one named last changes fastest.
Arguments:
- inputs: bfloat16 [16, 2048, 1024], P('dp', 'seq'), may hold values from -6 to 6
- cotangent: bfloat16 [16, 2048, 1024], P('dp', 'seq'), may hold values from -6 to 6
- segment_ids: int32 [16, 2048], P('dp'), may hold values from 0 to 21, as said below
- query_weight: bfloat16 [1024, 1024], P(('dp', 'seq')), may hold values from -0.1875 to 0.1875
- key_weight: bfloat16 [1024, 1024], P(('dp', 'seq')), may hold values from -0.1875 to 0.1875
- value_weight: bfloat16 [1024, 1024], P(('dp', 'seq')), may hold values from -0.1875 to 0.1875
- output_weight: bfloat16 [1024, 1024], P(('dp', 'seq')), may hold values from -0.1875 to 0.1875
- up_weight: bfloat16 [1024, 4096], P(('dp', 'seq')), may hold values from -0.1875 to 0.1875
- down_weight: bfloat16 [4096, 1024], P(('dp', 'seq')), may hold values from -0.09375 to 0.09375
- first_gain: float32 [1024], replicated, may hold values from 0.25 to 1.75
- first_shift: float32 [1024], replicated, may hold values from -1 to 1
- query_bias: float32 [1024], replicated, may hold values from -1 to 1
- value_bias: float32 [1024], replicated, may hold values from -1 to 1
- head_scale: float32 [16], replicated, may hold values from 0.3 to 3
- output_bias: float32 [1024], replicated, may hold values from -1 to 1
- post_gain: float32 [1024], replicated, may hold values from 0.25 to 1.75
- post_shift: float32 [1024], replicated, may hold values from -1 to 1
- second_gain: float32 [1024], replicated, may hold values from 0.25 to 1.75
- second_shift: float32 [1024], replicated, may hold values from -1 to 1
- up_bias: float32 [4096], replicated, may hold values from -1 to 1
- middle_gain: float32 [4096], replicated, may hold values from 0.25 to 1.75
- middle_shift: float32 [4096], replicated, may hold values from -1 to 1
- down_bias: float32 [1024], replicated, may hold values from -1 to 1
Outputs:
- layer_output: bfloat16 [16, 2048, 1024], P('dp', 'seq')
- input_grad: bfloat16 [16, 2048, 1024], P('dp', 'seq')
- query_weight_grad: float32 [1024, 1024], P(('dp', 'seq'))
- key_weight_grad: float32 [1024, 1024], P(('dp', 'seq'))
- value_weight_grad: float32 [1024, 1024], P(('dp', 'seq'))
- output_weight_grad: float32 [1024, 1024], P(('dp', 'seq'))
- up_weight_grad: float32 [1024, 4096], P(('dp', 'seq'))
- down_weight_grad: float32 [4096, 1024], P(('dp', 'seq'))
- first_gain_grad: float32 [1024], replicated
- first_shift_grad: float32 [1024], replicated
- query_bias_grad: float32 [1024], replicated
- value_bias_grad: float32 [1024], replicated
- head_scale_grad: float32 [16], replicated
- output_bias_grad: float32 [1024], replicated
- post_gain_grad: float32 [1024], replicated
- post_shift_grad: float32 [1024], replicated
- second_gain_grad: float32 [1024], replicated
- second_shift_grad: float32 [1024], replicated
- up_bias_grad: float32 [4096], replicated
- middle_gain_grad: float32 [4096], replicated
- middle_shift_grad: float32 [4096], replicated
- down_bias_grad: float32 [1024], replicated
Inputs may be any that keep to these rules, and one draw needn't show every extreme that they name: `segment_ids`: along each sequence the ids start at 0 and never fall; each document (a run of equal ids) has 60 to 800 positions, except the last of a sequence, which the sequence's end may cut short; in each sequence the first or the second document has exactly 800 positions; the last sequence reaches the largest id.
All inputs are finite; a program needn't handle non-finite values.
Results may differ from a plain program's by a relative error of at most 0.014.
Values may be sent and summed in bfloat16 or wider, within the bound.
A program may use at most 184 MiB of HBM per device.

v0:
```python
import jax
import jax.numpy as jnp
from jax import lax
from jax.sharding import PartitionSpec as P

EPSILON = 1e-05
MASKED = -1e30


def layer_norm(values, gain_vec, shift_vec):
    row_mean = jnp.mean(values, -1, keepdims=True)
    centred = values - row_mean
    spread = jnp.mean(centred * centred, -1, keepdims=True)
    return centred * lax.rsqrt(spread + EPSILON) * gain_vec + shift_vec


def exact_gelu(values):
    return jax.nn.gelu(values, approximate=False)


def matmul(left_side, right_side):
    return jnp.dot(left_side, right_side, preferred_element_type=jnp.float32)


def contract_rows(left_side, right_side):
    return lax.dot_general(
        left_side, right_side, (((0,), (0,)), ((), ())), preferred_element_type=jnp.float32
    )


def contract_last(left_side, right_side):
    return lax.dot_general(
        left_side, right_side, (((1,), (1,)), ((), ())), preferred_element_type=jnp.float32
    )


def split_heads(matrix, head_count):
    return matrix.reshape(matrix.shape[0], head_count, -1).transpose(1, 0, 2)


def join_heads(stacked):
    return stacked.transpose(1, 0, 2).reshape(stacked.shape[1], -1)


def head_scores(single_query_head, single_key_head, allowed, logit_scale_factor):
    score_matrix = contract_last(single_query_head, single_key_head) * logit_scale_factor
    return jnp.where(allowed, score_matrix, MASKED)


def local(
    inputs,
    cotangent,
    segment_ids,
    query_weight,
    key_weight,
    value_weight,
    output_weight,
    up_weight,
    down_weight,
    first_gain,
    first_shift,
    query_bias,
    value_bias,
    head_scale,
    output_bias,
    post_gain,
    post_shift,
    second_gain,
    second_shift,
    up_bias,
    middle_gain,
    middle_shift,
    down_bias,
):
    micro_count, row_count, model_width = inputs.shape
    hidden_width = up_bias.shape[0]
    head_count = head_scale.shape[0]
    logit_scale_factor = (model_width // head_count) ** (-0.5)
    seq_ranks = lax.axis_size("seq")
    rank_index = lax.axis_index("seq")
    length = row_count * seq_ranks
    query_place = rank_index * row_count + jnp.arange(row_count)
    causal = jnp.arange(length)[None, :] <= query_place[:, None]
    square = (model_width, model_width)
    matrix_sums = [
        jnp.zeros(square, jnp.float32),
        jnp.zeros(square, jnp.float32),
        jnp.zeros(square, jnp.float32),
        jnp.zeros(square, jnp.float32),
        jnp.zeros((model_width, hidden_width), jnp.float32),
        jnp.zeros((hidden_width, model_width), jnp.float32),
    ]
    vectors = (
        first_gain,
        first_shift,
        query_bias,
        value_bias,
        head_scale,
        output_bias,
        post_gain,
        post_shift,
        second_gain,
        second_shift,
        up_bias,
        middle_gain,
        middle_shift,
        down_bias,
    )
    vector_sums = [jnp.zeros_like(tensor) for tensor in vectors]
    outputs = []
    input_grads = []
    for micro_step in range(micro_count):
        tokens = inputs[micro_step].astype(jnp.float32)
        segment_row = segment_ids[micro_step]
        segment_query = lax.dynamic_slice_in_dim(segment_row, rank_index * row_count, row_count)
        attention_full = (
            lax.all_gather(query_weight, ("dp", "seq"), axis=0, tiled=True),
            lax.all_gather(key_weight, ("dp", "seq"), axis=0, tiled=True),
            lax.all_gather(value_weight, ("dp", "seq"), axis=0, tiled=True),
            lax.all_gather(output_weight, ("dp", "seq"), axis=0, tiled=True),
        )
        query_full, key_full, value_full, output_full = attention_full
        normed, first_back = jax.vjp(layer_norm, tokens, first_gain, first_shift)
        normed_low = normed.astype(jnp.bfloat16)
        query_low = (matmul(normed_low, query_full) + query_bias).astype(jnp.bfloat16)
        key_low = matmul(normed_low, key_full).astype(jnp.bfloat16)
        value_low = (matmul(normed_low, value_full) + value_bias).astype(jnp.bfloat16)
        key_all, value_all = (
            lax.all_gather(key_low, "seq", axis=0, tiled=True),
            lax.all_gather(value_low, "seq", axis=0, tiled=True),
        )
        allowed = causal & (segment_row[None, :] == segment_query[:, None])
        query_heads = split_heads(query_low, head_count)
        key_heads = split_heads(key_all, head_count)
        value_heads = split_heads(value_all, head_count)

        def attend(packed):
            single_query_head, single_key_head, single_value_head = packed
            score_matrix = head_scores(
                single_query_head, single_key_head, allowed, logit_scale_factor
            )
            largest = jnp.max(score_matrix, -1, keepdims=True)
            exponent = jnp.exp(score_matrix - largest)
            row_total = jnp.sum(exponent, -1, keepdims=True)
            weights_low = (exponent / row_total).astype(jnp.bfloat16)
            return (matmul(weights_low, single_value_head), (largest + jnp.log(row_total))[:, 0])

        attended, logsums = lax.map(attend, (query_heads, key_heads, value_heads))
        scaled_low = join_heads(attended * head_scale[:, None, None]).astype(jnp.bfloat16)
        branch = matmul(scaled_low, output_full) + output_bias
        posted, post_back = jax.vjp(layer_norm, branch, post_gain, post_shift)
        middle = tokens + posted
        feedforward_full = (
            lax.all_gather(up_weight, ("dp", "seq"), axis=0, tiled=True),
            lax.all_gather(down_weight, ("dp", "seq"), axis=0, tiled=True),
        )
        up_full, down_full = feedforward_full
        normed_two, second_back = jax.vjp(layer_norm, middle, second_gain, second_shift)
        second_low = normed_two.astype(jnp.bfloat16)
        upper_pre = matmul(second_low, up_full) + up_bias
        activated, gelu_back = jax.vjp(exact_gelu, upper_pre)
        mixed, middle_back = jax.vjp(layer_norm, activated, middle_gain, middle_shift)
        mixed_low = mixed.astype(jnp.bfloat16)
        output = middle + matmul(mixed_low, down_full) + down_bias
        outputs.append(output.astype(jnp.bfloat16))
        query_full, key_full, value_full, output_full = (
            lax.all_gather(query_weight, ("dp", "seq"), axis=0, tiled=True),
            lax.all_gather(key_weight, ("dp", "seq"), axis=0, tiled=True),
            lax.all_gather(value_weight, ("dp", "seq"), axis=0, tiled=True),
            lax.all_gather(output_weight, ("dp", "seq"), axis=0, tiled=True),
        )
        up_full, down_full = (
            lax.all_gather(up_weight, ("dp", "seq"), axis=0, tiled=True),
            lax.all_gather(down_weight, ("dp", "seq"), axis=0, tiled=True),
        )
        grad_low = cotangent[micro_step]
        grad_out = grad_low.astype(jnp.float32)
        grad_mixed = contract_last(grad_low, down_full)
        grad_activated, middle_gain_term, middle_shift_term = middle_back(grad_mixed)
        (grad_upper,) = gelu_back(grad_activated)
        upper_low = grad_upper.astype(jnp.bfloat16)
        grad_second = contract_last(upper_low, up_full)
        grad_middle_part, second_gain_term, second_shift_term = second_back(grad_second)
        grad_middle = grad_out + grad_middle_part
        grad_branch, post_gain_term, post_shift_term = post_back(grad_middle)
        branch_low = grad_branch.astype(jnp.bfloat16)
        grad_scaled = split_heads(contract_last(branch_low, output_full), head_count)
        head_term = jnp.sum(grad_scaled * attended, axis=(1, 2))
        grad_attended = (grad_scaled * head_scale[:, None, None]).astype(jnp.bfloat16)

        def attend_back(packed):
            single_query_head, single_key_head, single_value_head, grad_head, logsum = packed
            score_matrix = head_scores(
                single_query_head, single_key_head, allowed, logit_scale_factor
            )
            attention_probabilities = jnp.exp(score_matrix - logsum[:, None])
            weights_low = attention_probabilities.astype(jnp.bfloat16)
            grad_weights = contract_last(grad_head, single_value_head)
            grad_value = contract_rows(weights_low, grad_head)
            row_inner = jnp.sum(attention_probabilities * grad_weights, -1, keepdims=True)
            grad_scores = (attention_probabilities * (grad_weights - row_inner)).astype(
                jnp.bfloat16
            )
            grad_query = matmul(grad_scores, single_key_head) * logit_scale_factor
            grad_key = contract_rows(grad_scores, single_query_head) * logit_scale_factor
            return (grad_query, grad_key, grad_value)

        grad_queries, grad_keys, grad_values = lax.map(
            attend_back, (query_heads, key_heads, value_heads, grad_attended, logsums)
        )
        query_grad_low = join_heads(grad_queries).astype(jnp.bfloat16)
        key_sum, value_sum = (
            lax.psum_scatter(
                join_heads(grad_keys).astype(jnp.bfloat16), "seq", scatter_dimension=0, tiled=True
            ).astype(jnp.float32),
            lax.psum_scatter(
                join_heads(grad_values).astype(jnp.bfloat16), "seq", scatter_dimension=0, tiled=True
            ).astype(jnp.float32),
        )
        key_grad_low = key_sum.astype(jnp.bfloat16)
        value_grad_low = value_sum.astype(jnp.bfloat16)
        grad_normed = (
            contract_last(query_grad_low, query_full)
            + contract_last(key_grad_low, key_full)
            + contract_last(value_grad_low, value_full)
        )
        grad_tokens, first_gain_term, first_shift_term = first_back(grad_normed)
        input_grads.append((grad_middle + grad_tokens).astype(jnp.bfloat16))
        matrix_terms = (
            contract_rows(normed_low, query_grad_low),
            contract_rows(normed_low, key_grad_low),
            contract_rows(normed_low, value_grad_low),
            contract_rows(scaled_low, branch_low),
            contract_rows(second_low, upper_low),
            contract_rows(mixed_low, grad_low),
        )
        matrix_sums = [running + adding for running, adding in zip(matrix_sums, matrix_terms)]
        vector_terms = (
            first_gain_term,
            first_shift_term,
            jnp.sum(query_grad_low.astype(jnp.float32), 0),
            jnp.sum(value_grad_low.astype(jnp.float32), 0),
            head_term,
            jnp.sum(branch_low.astype(jnp.float32), 0),
            post_gain_term,
            post_shift_term,
            second_gain_term,
            second_shift_term,
            jnp.sum(upper_low.astype(jnp.float32), 0),
            middle_gain_term,
            middle_shift_term,
            jnp.sum(grad_out, 0),
        )
        vector_sums = [running + adding for running, adding in zip(vector_sums, vector_terms)]
    weight_parts = (
        lax.psum_scatter(matrix_sums[0], ("dp", "seq"), scatter_dimension=0, tiled=True),
        lax.psum_scatter(matrix_sums[1], ("dp", "seq"), scatter_dimension=0, tiled=True),
        lax.psum_scatter(matrix_sums[2], ("dp", "seq"), scatter_dimension=0, tiled=True),
        lax.psum_scatter(matrix_sums[3], ("dp", "seq"), scatter_dimension=0, tiled=True),
        lax.psum_scatter(matrix_sums[4], ("dp", "seq"), scatter_dimension=0, tiled=True),
        lax.psum_scatter(matrix_sums[5], ("dp", "seq"), scatter_dimension=0, tiled=True),
    )
    vector_parts = lax.psum(
        (
            vector_sums[0],
            vector_sums[1],
            vector_sums[2],
            vector_sums[3],
            vector_sums[4],
            vector_sums[5],
            vector_sums[6],
            vector_sums[7],
            vector_sums[8],
            vector_sums[9],
            vector_sums[10],
            vector_sums[11],
            vector_sums[12],
            vector_sums[13],
        ),
        ("dp", "seq"),
    )
    return (
        jnp.stack(outputs),
        jnp.stack(input_grads),
        weight_parts[0],
        weight_parts[1],
        weight_parts[2],
        weight_parts[3],
        weight_parts[4],
        weight_parts[5],
        vector_parts[0],
        vector_parts[1],
        vector_parts[2],
        vector_parts[3],
        vector_parts[4],
        vector_parts[5],
        vector_parts[6],
        vector_parts[7],
        vector_parts[8],
        vector_parts[9],
        vector_parts[10],
        vector_parts[11],
        vector_parts[12],
        vector_parts[13],
    )


def solution(mesh):
    in_specs = (
        P("dp", "seq", None),
        P("dp", "seq", None),
        P("dp", None),
        P(("dp", "seq"), None),
        P(("dp", "seq"), None),
        P(("dp", "seq"), None),
        P(("dp", "seq"), None),
        P(("dp", "seq"), None),
        P(("dp", "seq"), None),
        P(),
        P(),
        P(),
        P(),
        P(),
        P(),
        P(),
        P(),
        P(),
        P(),
        P(),
        P(),
        P(),
        P(),
    )
    out_specs = (
        P("dp", "seq", None),
        P("dp", "seq", None),
        P(("dp", "seq"), None),
        P(("dp", "seq"), None),
        P(("dp", "seq"), None),
        P(("dp", "seq"), None),
        P(("dp", "seq"), None),
        P(("dp", "seq"), None),
        P(),
        P(),
        P(),
        P(),
        P(),
        P(),
        P(),
        P(),
        P(),
        P(),
        P(),
        P(),
        P(),
        P(),
    )
    return jax.shard_map(local, mesh=mesh, in_specs=in_specs, out_specs=out_specs, check_vma=False)
```

profile of v0, /device:TPU:0, one launch (start us, length us, event | category | flops | bytes accessed | tf_op | source)
XLA Modules:
  0.0 2929.8 jit_solution(12358509383623044732)
XLA Ops:
  12.2 57.9 %all-gather.13.cloned.1.call-done = bf16[1024,1024]{1,0:T(8,128)(2,1)} async-done(((bf16[32,1024]{1,0:T(8,128)(2,1)}), bf16[1024,1024]{1,0:T(8,128)(2,1)}) %all-gather.13.cloned.1.call-update) | async-done | bytes 2097168 | tf_op jit(solution)/shard_map/all_gather | solution.py:118
  74.1 54.2 %all-gather.17.cloned.1.call-done = bf16[1024,1024]{1,0:T(8,128)(2,1)} async-done(((bf16[32,1024]{1,0:T(8,128)(2,1)}), bf16[1024,1024]{1,0:T(8,128)(2,1)}) %all-gather.17.cloned.1.call-update) | async-done | bytes 2097168 | tf_op jit(solution)/shard_map/all_gather | solution.py:119
  143.8 42.6 %all-gather.11.cloned.1.call-done = bf16[1024,1024]{1,0:T(8,128)(2,1)} async-done(((bf16[32,1024]{1,0:T(8,128)(2,1)}), bf16[1024,1024]{1,0:T(8,128)(2,1)}) %all-gather.11.cloned.1.call-update) | async-done | bytes 2097168 | tf_op jit(solution)/shard_map/all_gather | solution.py:117
  202.6 64.8 %all-gather.15.cloned.1.call-done = bf16[2048,1024]{1,0:T(8,128)(2,1)} async-done(((bf16[512,1024]{1,0:T(8,128)(2,1)}), bf16[2048,1024]{1,0:T(8,128)(2,1)}) %all-gather.15.cloned.1.call-update) | async-done | bytes 4194320 | tf_op jit(solution)/shard_map/all_gather | solution.py:129
  282.4 65.7 %all-gather.19.cloned.1.call-done = bf16[2048,1024]{1,0:T(8,128)(2,1)} async-done(((bf16[512,1024]{1,0:T(8,128)(2,1)}), bf16[2048,1024]{1,0:T(8,128)(2,1)}) %all-gather.19.cloned.1.call-update) | async-done | bytes 4194320 | tf_op jit(solution)/shard_map/all_gather | solution.py:130
  364.8 94.9 %while.56 = (s32[]{:T(128)}, f32[16,512,64]{1,2,0:T(8,128)}, f32[16,512]{1,0:T(8,128)S(1)}, bf16[16,512,64]{2,1,0:T(8,128)(2,1)}, bf16[16,2048,64]{2,1,0:T(8,128...) while((s32[]{:T(128)}, f32[16,512,64]{1,2,0:T(8,128)}, ...), condition=%wide.region_5.6_spmd.clone, body=%wide.region_2.5_spmd.clone.sunk | while | flops 279969280 | bytes 13928569 | solution.py:148
  474.7 34.9 %all-gather.29.cloned.1.call-done = bf16[2048,1024]{1,0:T(8,128)(2,1)} async-done(((bf16[512,1024]{1,0:T(8,128)(2,1)}), bf16[2048,1024]{1,0:T(8,128)(2,1)}) %all-gather.29.cloned.1.call-update) | async-done | bytes 4194320 | tf_op jit(solution)/shard_map/all_gather | solution.py:130
  526.2 95.4 %while.57 = (s32[]{:T(128)}, f32[16,512,64]{1,2,0:T(8,128)}, f32[16,512]{1,0:T(8,128)S(1)}, bf16[16,512,64]{2,1,0:T(8,128)(2,1)}, bf16[16,2048,64]{2,1,0:T(8,128...) while((s32[]{:T(128)}, f32[16,512,64]{1,2,0:T(8,128)}, ...), condition=%wide.region_17.18_spmd.clone, body=%wide.region_14.17_spmd.clone.sunk | while | flops 279969280 | bytes 13928569 | solution.py:148
  654.2 48.7 %fusion.197 = (f32[512]{0:T(512)S(1)}, f32[512,4096]{1,0:T(8,128)}, f32[512,4096]{1,0:T(8,128)}, f32[512]{0:T(512)S(1)}, f32[512,4096]{1,0:T(8,128)}, /*index=5*/f32[512,4096]{1,0:T(8,128)}, f32[512,4096]{1,0:T(8,128)}) fusion(f32[4096]{0:T(1024)S(1)} %copy-done.107, f32[512,4096]{1,0:T(8,128)S(1)} %fusion.178, ...), kind=kOutput, calls=%fused_computation.343 | convolution fusion | flops 4574411776 | bytes 60850176 | tf_op jit(solution)/shard_map/dot_general | solution.py:22
  703.0 21.8 all-gather.25.cloned.1.call-done
  736.4 17.3 multiply_reduce_fusion.5
  768.9 24.0 convert_reduce_fusion
  834.2 178.0 %while.59 = (s32[]{:T(128)}, bf16[16,512,64]{1,2,0:T(8,128)(2,1)S(1)}, bf16[16,2048,64]{1,2,0:T(8,128)(2,1)}, bf16[16,2048,64]{1,2,0:T(8,128)(2,1)}, bf16[16,512...) while((s32[]{:T(128)}, ...), condition=%wide.region_45.46_spmd.clone, body=%wide.region_43.45_spmd.clone.sunk | while | flops 683834880 | bytes 34630792 | solution.py:208
  1017.3 178.0 %while.58 = (s32[]{:T(128)}, bf16[16,512,64]{1,2,0:T(8,128)(2,1)S(1)}, bf16[16,2048,64]{1,2,0:T(8,128)(2,1)}, bf16[16,2048,64]{1,2,0:T(8,128)(2,1)}, bf16[16,512...) while((s32[]{:T(128)}, ...), condition=%wide.region_32.33_spmd.clone, body=%wide.region_30.32_spmd.clone.sunk | while | flops 683834880 | bytes 34630792 | solution.py:208
  1233.7 37.2 %reduce-scatter.11.cloned.1.call-done = bf16[512,1024]{0,1:T(8,128)(2,1)} async-done(((bf16[2048,1024]{0,1:T(8,128)(2,1)}), bf16[512,1024]{0,1:T(8,128)(2,1)}) %reduce-scatter.11.cloned.1.call-update) | async-done | bytes 1048592 | tf_op jit(solution)/shard_map/reduce_scatter | solution.py:213
  1275.5 75.0 %reduce-scatter.17.cloned.1.call-done = bf16[512,1024]{0,1:T(8,128)(2,1)} async-done(((bf16[2048,1024]{0,1:T(8,128)(2,1)}), bf16[512,1024]{0,1:T(8,128)(2,1)}) %reduce-scatter.17.cloned.1.call-update) | async-done | bytes 1048592 | tf_op jit(solution)/shard_map/reduce_scatter | solution.py:216
  1356.3 73.7 %reduce-scatter.13.cloned.1.call-done = bf16[512,1024]{0,1:T(8,128)(2,1)} async-done(((bf16[2048,1024]{0,1:T(8,128)(2,1)}), bf16[512,1024]{0,1:T(8,128)(2,1)}) %reduce-scatter.13.cloned.1.call-update) | async-done | bytes 1048592 | tf_op jit(solution)/shard_map/reduce_scatter | solution.py:216
  1538.3 43.6 %reduce-scatter.19.cloned.1.call-done = f32[32,1024]{1,0:T(8,128)} async-done(((f32[1024,1024]{1,0:T(8,128)}), f32[32,1024]{1,0:T(8,128)}) %reduce-scatter.19.cloned.1.call-update) | async-done | bytes 131088 | tf_op jit(solution)/shard_map/reduce_scatter | solution.py:256
  1581.9 151.3 %reduce-scatter.25.cloned.1.call-done = f32[32,1024]{1,0:T(8,128)} async-done(((f32[1024,1024]{1,0:T(8,128)}), f32[32,1024]{1,0:T(8,128)}) %reduce-scatter.25.cloned.1.call-update) | async-done | bytes 131088 | tf_op jit(solution)/shard_map/reduce_scatter | solution.py:259
  1733.2 140.7 %all-reduce.3.cloned.1.call-done = (f32[1024]{0:T(1024)}, f32[1024]{0:T(1024)}, f32[1024]{0:T(1024)}, f32[1024]{0:T(1024)}, f32[16]{0:T(128)}, /*index=5*/f32[10...) async-done(((f32[1024]{0:T(1024)}, f32[1024]{0:T(1024)}, ...) | async-done | bytes 90192 | tf_op jit(solution)/shard_map/psum | solution.py:263
  1873.9 153.3 %reduce-scatter.21.cloned.1.call-done = f32[32,1024]{1,0:T(8,128)} async-done(((f32[1024,1024]{1,0:T(8,128)}), f32[32,1024]{1,0:T(8,128)}) %reduce-scatter.21.cloned.1.call-update) | async-done | bytes 131088 | tf_op jit(solution)/shard_map/reduce_scatter | solution.py:257
  2027.2 150.5 %reduce-scatter.23.cloned.1.call-done = f32[32,1024]{1,0:T(8,128)} async-done(((f32[1024,1024]{1,0:T(8,128)}), f32[32,1024]{1,0:T(8,128)}) %reduce-scatter.23.cloned.1.call-update) | async-done | bytes 131088 | tf_op jit(solution)/shard_map/reduce_scatter | solution.py:258
  2177.7 362.3 %reduce-scatter.27.cloned.1.call-done = f32[32,4096]{1,0:T(8,128)} async-done(((f32[1024,4096]{1,0:T(8,128)}), f32[32,4096]{1,0:T(8,128)}) %reduce-scatter.27.cloned.1.call-update) | async-done | bytes 524304 | tf_op jit(solution)/shard_map/reduce_scatter | solution.py:260
  2540.0 364.8 %reduce-scatter.29.cloned.1.call-done = f32[128,1024]{1,0:T(8,128)} async-done(((f32[4096,1024]{1,0:T(8,128)}), f32[128,1024]{1,0:T(8,128)}) %reduce-scatter.29.cloned.1.call-update) | async-done | bytes 524304 | tf_op jit(solution)/shard_map/reduce_scatter | solution.py:261
  (840 shorter events, 927.2 us)
Async XLA Ops:
  7.2 62.9 %all-gather.13.cloned.1.call-start = ((), (), s32[]{:S(2)}) async-start(), calls=%async_computation.11 | async-start | bytes 2162688 | tf_op jit(solution)/shard_map/all_gather | solution.py:118
  7.9 120.3 %all-gather.17.cloned.1.call-start = ((), (), s32[]{:S(2)}) async-start(), calls=%async_computation.13 | async-start | bytes 2162688 | tf_op jit(solution)/shard_map/all_gather | solution.py:119
  8.7 177.7 %all-gather.11.cloned.1.call-start = ((), (), s32[]{:S(2)}) async-start(), calls=%async_computation.10 | async-start | bytes 2162688 | tf_op jit(solution)/shard_map/all_gather | solution.py:117
  9.4 258.0 %all-gather.15.cloned.1.call-start = ((), (), s32[]{:S(2)}) async-start(), calls=%async_computation.12 | async-start | bytes 5242880 | tf_op jit(solution)/shard_map/all_gather | solution.py:129
  11.4 183.9 %copy-start.53 = (f32[512]{0:T(512)}, f32[512]{0:T(512)S(1)}, u32[]{:S(2)}) copy-start(f32[512]{0:T(512)S(1)} %get-tuple-element.588) | copy-start | bytes 6148
  74.0 274.1 %all-gather.19.cloned.1.call-start = ((), (), s32[]{:S(2)}) async-start(), calls=%async_computation.14 | async-start | bytes 5242880 | tf_op jit(solution)/shard_map/all_gather | solution.py:130
  132.1 327.6 %all-gather.27.cloned.1.call-start = ((), (), s32[]{:S(2)}) async-start(), calls=%async_computation.18 | async-start | bytes 5242880 | tf_op jit(solution)/shard_map/all_gather | solution.py:129
  136.2 373.5 %all-gather.29.cloned.1.call-start = ((), (), s32[]{:S(2)}) async-start(), calls=%async_computation.19 | async-start | bytes 5242880 | tf_op jit(solution)/shard_map/all_gather | solution.py:130
  140.2 486.0 %all-gather.21.cloned.1.call-start = ((), (), s32[]{:S(2)}) async-start(), calls=%async_computation.15 | async-start | bytes 2162688 | tf_op jit(solution)/shard_map/all_gather | solution.py:120
  140.9 505.4 %all-gather.23.cloned.1.call-start = ((), (), s32[]{:S(2)}) async-start(), calls=%async_computation.16 | async-start | bytes 8650752 | tf_op jit(solution)/shard_map/all_gather | solution.py:154
  141.7 583.1 %all-gather.25.cloned.1.call-start = ((), (), s32[]{:S(2)}) async-start(), calls=%async_computation.17 | async-start | bytes 8650752 | tf_op jit(solution)/shard_map/all_gather | solution.py:155
  142.3 1086.9 %reduce-scatter.15.cloned.1.call-start = ((), (), s32[]{:S(2)}) async-start(), calls=%async_computation.22 | async-start | bytes 5242880 | tf_op jit(solution)/shard_map/reduce_scatter | solution.py:213
  634.5 179.4 %copy-start.95 = (f32[512]{0:T(512)}, f32[512]{0:T(512)S(1)}, u32[]{:S(2)}) copy-start(f32[512]{0:T(512)S(1)} %broadcast_multiply_fusion.5) | copy-start | bytes 6148
  636.0 177.8 %copy-start.115 = (f32[512]{0:T(512)}, f32[512]{0:T(512)S(1)}, u32[]{:S(2)}) copy-start(f32[512]{0:T(512)S(1)} %fusion.168) | copy-start | bytes 6148
  1012.2 258.7 %reduce-scatter.11.cloned.1.call-start = ((), (), s32[]{:S(2)}) async-start(), calls=%async_computation.20 | async-start | bytes 5242880 | tf_op jit(solution)/shard_map/reduce_scatter | solution.py:213
  1196.3 154.2 %reduce-scatter.17.cloned.1.call-start = ((), (), s32[]{:S(2)}) async-start(), calls=%async_computation.23 | async-start | bytes 5242880 | tf_op jit(solution)/shard_map/reduce_scatter | solution.py:216
  1197.0 233.0 %reduce-scatter.13.cloned.1.call-start = ((), (), s32[]{:S(2)}) async-start(), calls=%async_computation.21 | async-start | bytes 5242880 | tf_op jit(solution)/shard_map/reduce_scatter | solution.py:216
  1197.6 384.3 %reduce-scatter.19.cloned.1.call-start = ((), (), s32[]{:S(2)}) async-start(), calls=%async_computation.24 | async-start | bytes 4325376 | tf_op jit(solution)/shard_map/reduce_scatter | solution.py:256
  1205.0 528.2 %reduce-scatter.25.cloned.1.call-start = ((), (), s32[]{:S(2)}) async-start(), calls=%async_computation.27 | async-start | bytes 4325376 | tf_op jit(solution)/shard_map/reduce_scatter | solution.py:259
  1211.7 662.2 %all-reduce.3.cloned.1.call-start = ((), (), s32[]{:S(2)}) async-start(), calls=%async_computation.30 | async-start | bytes 181248 | tf_op jit(solution)/shard_map/psum | solution.py:263
  1440.7 586.5 %reduce-scatter.21.cloned.1.call-start = ((), (), s32[]{:S(2)}) async-start(), calls=%async_computation.25 | async-start | bytes 4325376 | tf_op jit(solution)/shard_map/reduce_scatter | solution.py:257
  1447.3 730.4 %reduce-scatter.23.cloned.1.call-start = ((), (), s32[]{:S(2)}) async-start(), calls=%async_computation.26 | async-start | bytes 4325376 | tf_op jit(solution)/shard_map/reduce_scatter | solution.py:258
  1453.7 1086.3 %reduce-scatter.27.cloned.1.call-start = ((), (), s32[]{:S(2)}) async-start(), calls=%async_computation.28 | async-start | bytes 17301504 | tf_op jit(solution)/shard_map/reduce_scatter | solution.py:260
  1479.8 1425.1 %reduce-scatter.29.cloned.1.call-start = ((), (), s32[]{:S(2)}) async-start(), calls=%async_computation.29 | async-start | bytes 17301504 | tf_op jit(solution)/shard_map/reduce_scatter | solution.py:261
  (131 other events, 2036.4 us)
Sparse Core Ops, SparseCore 0:
  10.9 59.0 all-gather.12
  73.0 55.1 all-gather.16
  131.2 55.1 all-gather.10
  187.8 79.5 all-gather.14
  268.9 79.2 all-gather.18
  349.5 79.2 all-gather.26
  430.4 79.2 all-gather.28
  512.5 54.8 all-gather.20
  570.4 75.9 all-gather.22
  649.1 75.6 all-gather.24
  1012.4 75.4 reduce-scatter.14
  1195.5 75.4 reduce-scatter.10
  1273.2 77.2 reduce-scatter.16
  1352.7 77.2 reduce-scatter.12
  1432.7 149.1 reduce-scatter.18
  1584.6 148.5 reduce-scatter.24
  1740.6 133.1 all-reduce.2
  1876.6 150.5 reduce-scatter.20
  2030.0 147.6 reduce-scatter.22
  2180.4 359.5 reduce-scatter.26
  2542.9 361.9 reduce-scatter.28
where the time goes:
time: 2950 us; the launch traced here: 2930 us
  waiting for transfers between devices  1910 us (65%)
  matrix products  750 us (25%)
  local copies, waits for them, and re-layouts  137 us (5%)
  other arithmetic  113 us (4%)
    reduce_scatter x1, waiting for transfers between devices, local(): lax.psum_scatter(matrix_sums[5], ('dp', 'seq'), scatter_dimension=0, tile...  365 us
    reduce_scatter x1, waiting for transfers between devices, local(): lax.psum_scatter(matrix_sums[4], ('dp', 'seq'), scatter_dimension=0, tile...  362 us
    dot_general x108, matrix products, contract_last(): lax.dot_general(left_side, right_side, (((1,), (1,)), ((), ())), preferre...  309 us
    dot_general x76, matrix products, matmul(): return jnp.dot(left_side, right_side, preferred_element_type=jnp.float32)  254 us
    dot_general x76, matrix products, contract_rows(): lax.dot_general(left_side, right_side, (((0,), (0,)), ((), ())), preferre...  187 us
    reduce_scatter x1, waiting for transfers between devices, local(): lax.psum_scatter(matrix_sums[1], ('dp', 'seq'), scatter_dimension=0, tile...  153 us
    reduce_scatter x1, waiting for transfers between devices, local(): lax.psum_scatter(matrix_sums[3], ('dp', 'seq'), scatter_dimension=0, tile...  151 us
    reduce_scatter x1, waiting for transfers between devices, local(): lax.psum_scatter(matrix_sums[2], ('dp', 'seq'), scatter_dimension=0, tile...  151 us
  transfers between devices with their start and end apart: 21, of which 18 were waited for; matrix products, arithmetic and copies ran while one was open for 23% of the time, Pallas kernels for 0%

commit v1 on v0

--- a/solution.py
+++ b/solution.py
@@ -125,9 +125,22 @@
         query_low = (matmul(normed_low, query_full) + query_bias).astype(jnp.bfloat16)
         key_low = matmul(normed_low, key_full).astype(jnp.bfloat16)
         value_low = (matmul(normed_low, value_full) + value_bias).astype(jnp.bfloat16)
+
+        def levels_all_see(arr):
+            found_now = jax.lax.axis_size("seq")
+            after = jax.lax.axis_index("seq")
+            next_value, h_now, carry_out = (found_now, after, arr.shape[0])
+            side_arr, u1 = (arr, 1)
+            while u1 < next_value:
+                answer = tuple(((dev, (dev - u1) % next_value) for dev in range(next_value)))
+                plain = jax.lax.ppermute(side_arr, "seq", answer)
+                side_arr = jnp.concatenate([side_arr, plain], axis=0)
+                u1 = 2 * u1
+            return jnp.roll(side_arr, h_now * carry_out, axis=0)
+
         key_all, value_all = (
             lax.all_gather(key_low, "seq", axis=0, tiled=True),
-            lax.all_gather(value_low, "seq", axis=0, tiled=True),
+            levels_all_see(value_low),
         )
         allowed = causal & (segment_row[None, :] == segment_query[:, None])
         query_heads = split_heads(query_low, head_count)

time: 2950 us -> 2980 us (1.010)
    all_gather x1, waiting for transfers between devices: 42.6 us -> 200 us  [local(): lax.all_gather(query_weight, ('dp', 'seq'), axis=0, tiled=True)]
    all_gather x2 -> x0, waiting for transfers between devices: 101 us -> none  [local(): lax.all_gather(value_low, 'seq', axis=0, tiled=True)]
    all_gather x2, waiting for transfers between devices: 64.8 us -> 12.2 us  [local(): lax.all_gather(key_low, 'seq', axis=0, tiled=True)]
    ppermute x0 -> x4, waiting for transfers between devices: none -> 41.4 us  [levels_all_see(): plain = jax.lax.ppermute(side_arr, 'seq', answer)]
    unnamed x289 -> x299, local copies, waits for them, and re-layouts: 69 us -> 68.8 us
  transfers between devices with their start and end apart: 21 -> 23, of which waited for: 18 -> 17; matrix products, arithmetic and copies ran while one was open for 23% -> 24% of each run, Pallas kernels for 0% -> 0%
where the time goes in v1:
time: 2980 us; the launch traced here: 2970 us
  waiting for transfers between devices  1920 us (64%)
  matrix products  746 us (25%)
  other arithmetic  142 us (5%)
  local copies, waits for them, and re-layouts  136 us (5%)
    reduce_scatter x1, waiting for transfers between devices, local(): lax.psum_scatter(matrix_sums[5], ('dp', 'seq'), scatter_dimension=0, tile...  365 us
    reduce_scatter x1, waiting for transfers between devices, local(): lax.psum_scatter(matrix_sums[4], ('dp', 'seq'), scatter_dimension=0, tile...  362 us
    dot_general x108, matrix products, contract_last(): lax.dot_general(left_side, right_side, (((1,), (1,)), ((), ())), preferre...  309 us
    dot_general x76, matrix products, matmul(): return jnp.dot(left_side, right_side, preferred_element_type=jnp.float32)  250 us
    all_gather x1, waiting for transfers between devices, local(): lax.all_gather(query_weight, ('dp', 'seq'), axis=0, tiled=True)  200 us
    dot_general x76, matrix products, contract_rows(): lax.dot_general(left_side, right_side, (((0,), (0,)), ((), ())), preferre...  187 us
    reduce_scatter x1, waiting for transfers between devices, local(): lax.psum_scatter(matrix_sums[1], ('dp', 'seq'), scatter_dimension=0, tile...  153 us
    reduce_scatter x1, waiting for transfers between devices, local(): lax.psum_scatter(matrix_sums[3], ('dp', 'seq'), scatter_dimension=0, tile...  151 us
  transfers between devices with their start and end apart: 23, of which 17 were waited for; matrix products, arithmetic and copies ran while one was open for 24% of the time, Pallas kernels for 0%

profile of v1, /device:TPU:0, one launch (start us, length us, event | category | flops | bytes accessed | tf_op | source)
XLA Modules:
  0.0 2966.1 jit_solution(14889374191115359948)
XLA Ops:
  12.2 57.9 %all-gather.11.cloned.1.call-done = bf16[1024,1024]{1,0:T(8,128)(2,1)} async-done(((bf16[32,1024]{1,0:T(8,128)(2,1)}), bf16[1024,1024]{1,0:T(8,128)(2,1)}) %all-gather.11.cloned.1.call-update) | async-done | bytes 2097168 | tf_op jit(solution)/shard_map/all_gather | solution.py:118
  79.3 48.9 %all-gather.15.cloned.1.call-done = bf16[1024,1024]{1,0:T(8,128)(2,1)} async-done(((bf16[32,1024]{1,0:T(8,128)(2,1)}), bf16[1024,1024]{1,0:T(8,128)(2,1)}) %all-gather.15.cloned.1.call-update) | async-done | bytes 2097168 | tf_op jit(solution)/shard_map/all_gather | solution.py:119
  134.9 23.8 collective-permute-done
  163.5 17.6 collective-permute-done.2
  184.8 199.9 %all-gather.9.cloned.1.call-done = bf16[1024,1024]{1,0:T(8,128)(2,1)} async-done(((bf16[32,1024]{1,0:T(8,128)(2,1)}), bf16[1024,1024]{1,0:T(8,128)(2,1)}) %all-gather.9.cloned.1.call-update) | async-done | bytes 2097168 | tf_op jit(solution)/shard_map/all_gather | solution.py:117
  482.3 94.8 %while.56 = (s32[]{:T(128)}, f32[16,512,64]{1,2,0:T(8,128)}, f32[16,512]{1,0:T(8,128)S(1)}, bf16[16,512,64]{2,1,0:T(8,128)(2,1)}, bf16[16,2048,64]{2,1,0:T(8,128...) while((s32[]{:T(128)}, f32[16,512,64]{1,2,0:T(8,128)}, ...), condition=%wide.region_5.7_spmd.clone, body=%wide.region_2.6_spmd.clone.sunk | while | flops 279969280 | bytes 13928569 | solution.py:161
  593.6 95.5 %while.57 = (s32[]{:T(128)}, f32[16,512,64]{1,2,0:T(8,128)}, f32[16,512]{1,0:T(8,128)S(1)}, bf16[16,512,64]{2,1,0:T(8,128)(2,1)}, bf16[16,2048,64]{2,1,0:T(8,128...) while((s32[]{:T(128)}, f32[16,512,64]{1,2,0:T(8,128)}, ...), condition=%wide.region_17.19_spmd.clone, body=%wide.region_14.18_spmd.clone.sunk | while | flops 279969280 | bytes 13928569 | solution.py:161
  711.5 48.5 %fusion.207 = (f32[512]{0:T(512)S(1)}, f32[512,4096]{1,0:T(8,128)}, f32[512,4096]{1,0:T(8,128)}, f32[512]{0:T(512)S(1)}, f32[512,4096]{1,0:T(8,128)}, /*index=5*/f32[512,4096]{1,0:T(8,128)}, f32[512,4096]{1,0:T(8,128)}) fusion(f32[4096]{0:T(1024)S(1)} %copy-done.112, f32[512,4096]{1,0:T(8,128)S(1)} %fusion.188, ...), kind=kOutput, calls=%fused_computation.367 | convolution fusion | flops 4574411776 | bytes 60850176 | tf_op jit(solution)/shard_map/dot_general | solution.py:22
  773.3 17.3 multiply_reduce_fusion.5
  790.7 15.1 multiply_reduce_fusion.2
  805.8 24.0 convert_reduce_fusion
  871.1 177.9 %while.59 = (s32[]{:T(128)}, bf16[16,512,64]{1,2,0:T(8,128)(2,1)S(1)}, bf16[16,2048,64]{1,2,0:T(8,128)(2,1)}, bf16[16,2048,64]{1,2,0:T(8,128)(2,1)}, bf16[16,512...) while((s32[]{:T(128)}, ...), condition=%wide.region_45.47_spmd.clone, body=%wide.region_43.46_spmd.clone.sunk | while | flops 683834880 | bytes 34630792 | solution.py:221
  1054.1 177.8 %while.58 = (s32[]{:T(128)}, bf16[16,512,64]{1,2,0:T(8,128)(2,1)S(1)}, bf16[16,2048,64]{1,2,0:T(8,128)(2,1)}, bf16[16,2048,64]{1,2,0:T(8,128)(2,1)}, bf16[16,512...) while((s32[]{:T(128)}, ...), condition=%wide.region_32.34_spmd.clone, body=%wide.region_30.33_spmd.clone.sunk | while | flops 683834880 | bytes 34630792 | solution.py:221
  1270.3 37.2 %reduce-scatter.11.cloned.1.call-done = bf16[512,1024]{0,1:T(8,128)(2,1)} async-done(((bf16[2048,1024]{0,1:T(8,128)(2,1)}), bf16[512,1024]{0,1:T(8,128)(2,1)}) %reduce-scatter.11.cloned.1.call-update) | async-done | bytes 1048592 | tf_op jit(solution)/shard_map/reduce_scatter | solution.py:226
  1312.0 75.1 %reduce-scatter.17.cloned.1.call-done = bf16[512,1024]{0,1:T(8,128)(2,1)} async-done(((bf16[2048,1024]{0,1:T(8,128)(2,1)}), bf16[512,1024]{0,1:T(8,128)(2,1)}) %reduce-scatter.17.cloned.1.call-update) | async-done | bytes 1048592 | tf_op jit(solution)/shard_map/reduce_scatter | solution.py:229
  1392.9 73.7 %reduce-scatter.13.cloned.1.call-done = bf16[512,1024]{0,1:T(8,128)(2,1)} async-done(((bf16[2048,1024]{0,1:T(8,128)(2,1)}), bf16[512,1024]{0,1:T(8,128)(2,1)}) %reduce-scatter.13.cloned.1.call-update) | async-done | bytes 1048592 | tf_op jit(solution)/shard_map/reduce_scatter | solution.py:229
  1531.4 14.9 convolution_add_fusion.1
  1574.8 44.2 %reduce-scatter.19.cloned.1.call-done = f32[32,1024]{1,0:T(8,128)} async-done(((f32[1024,1024]{1,0:T(8,128)}), f32[32,1024]{1,0:T(8,128)}) %reduce-scatter.19.cloned.1.call-update) | async-done | bytes 131088 | tf_op jit(solution)/shard_map/reduce_scatter | solution.py:269
  1619.1 150.8 %reduce-scatter.25.cloned.1.call-done = f32[32,1024]{1,0:T(8,128)} async-done(((f32[1024,1024]{1,0:T(8,128)}), f32[32,1024]{1,0:T(8,128)}) %reduce-scatter.25.cloned.1.call-update) | async-done | bytes 131088 | tf_op jit(solution)/shard_map/reduce_scatter | solution.py:272
  1769.9 141.3 %all-reduce.3.cloned.1.call-done = (f32[1024]{0:T(1024)}, f32[1024]{0:T(1024)}, f32[1024]{0:T(1024)}, f32[1024]{0:T(1024)}, f32[16]{0:T(128)}, /*index=5*/f32[10...) async-done(((f32[1024]{0:T(1024)}, f32[1024]{0:T(1024)}, ...) | async-done | bytes 90192 | tf_op jit(solution)/shard_map/psum | solution.py:276
  1911.2 153.1 %reduce-scatter.21.cloned.1.call-done = f32[32,1024]{1,0:T(8,128)} async-done(((f32[1024,1024]{1,0:T(8,128)}), f32[32,1024]{1,0:T(8,128)}) %reduce-scatter.21.cloned.1.call-update) | async-done | bytes 131088 | tf_op jit(solution)/shard_map/reduce_scatter | solution.py:270
  2064.2 150.3 %reduce-scatter.23.cloned.1.call-done = f32[32,1024]{1,0:T(8,128)} async-done(((f32[1024,1024]{1,0:T(8,128)}), f32[32,1024]{1,0:T(8,128)}) %reduce-scatter.23.cloned.1.call-update) | async-done | bytes 131088 | tf_op jit(solution)/shard_map/reduce_scatter | solution.py:271
  2214.6 362.2 %reduce-scatter.27.cloned.1.call-done = f32[32,4096]{1,0:T(8,128)} async-done(((f32[1024,4096]{1,0:T(8,128)}), f32[32,4096]{1,0:T(8,128)}) %reduce-scatter.27.cloned.1.call-update) | async-done | bytes 524304 | tf_op jit(solution)/shard_map/reduce_scatter | solution.py:273
  2576.8 364.8 %reduce-scatter.29.cloned.1.call-done = f32[128,1024]{1,0:T(8,128)} async-done(((f32[4096,1024]{1,0:T(8,128)}), f32[128,1024]{1,0:T(8,128)}) %reduce-scatter.29.cloned.1.call-update) | async-done | bytes 524304 | tf_op jit(solution)/shard_map/reduce_scatter | solution.py:274
  (856 shorter events, 927.9 us)
Async XLA Ops:
  7.2 62.9 %all-gather.11.cloned.1.call-start = ((), (), s32[]{:S(2)}) async-start(), calls=%async_computation.11 | async-start | bytes 2162688 | tf_op jit(solution)/shard_map/all_gather | solution.py:118
  7.9 120.3 %all-gather.15.cloned.1.call-start = ((), (), s32[]{:S(2)}) async-start(), calls=%async_computation.13 | async-start | bytes 2162688 | tf_op jit(solution)/shard_map/all_gather | solution.py:119
  8.7 376.0 %all-gather.9.cloned.1.call-start = ((), (), s32[]{:S(2)}) async-start(), calls=%async_computation.10 | async-start | bytes 2162688 | tf_op jit(solution)/shard_map/all_gather | solution.py:117
  9.4 456.3 %all-gather.13.cloned.1.call-start = ((), (), s32[]{:S(2)}) async-start(), calls=%async_computation.12 | async-start | bytes 5242880 | tf_op jit(solution)/shard_map/all_gather | solution.py:142
  11.4 380.4 %copy-start.58 = (f32[512]{0:T(512)}, f32[512]{0:T(512)S(1)}, u32[]{:S(2)}) copy-start(f32[512]{0:T(512)S(1)} %get-tuple-element.589) | copy-start | bytes 6148
  74.0 503.2 %all-gather.23.cloned.1.call-start = ((), (), s32[]{:S(2)}) async-start(), calls=%async_computation.17 | async-start | bytes 5242880 | tf_op jit(solution)/shard_map/all_gather | solution.py:142
  78.0 615.7 %all-gather.17.cloned.1.call-start = ((), (), s32[]{:S(2)}) async-start(), calls=%async_computation.14 | async-start | bytes 2162688 | tf_op jit(solution)/shard_map/all_gather | solution.py:120
  78.5 625.0 %all-gather.19.cloned.1.call-start = ((), (), s32[]{:S(2)}) async-start(), calls=%async_computation.15 | async-start | bytes 8650752 | tf_op jit(solution)/shard_map/all_gather | solution.py:167
  79.3 682.5 %all-gather.21.cloned.1.call-start = ((), (), s32[]{:S(2)}) async-start(), calls=%async_computation.16 | async-start | bytes 8650752 | tf_op jit(solution)/shard_map/all_gather | solution.py:168
  131.3 27.5 collective-permute-start
  134.9 46.3 %collective-permute-start.2 = (bf16[512,1024]{1,0:T(8,128)(2,1)S(1)}, bf16[512,1024]{1,0:T(8,128)(2,1)}, u32[]{:S(2)}, u32[]{:S(2)}) collective-permute-start(bf16[512,1024]{1,0:T(8,128)(2,1)S(1)} %add_convert_fusion.10), channel_id=1, source_target_pairs={{0,3},{1,0},{2,1},{3,2},{4,7},{5,4},{6,5},{7,6},{8,11},{9,8},{10,9... | collective-permute-start | bytes 3145736 | tf_op jit(solution)/shard_map/ppermute | solution.py:136
  160.4 238.8 %collective-permute-start.1 = (bf16[1024,1024]{1,0:T(8,128)(2,1)}, bf16[1024,1024]{1,0:T(8,128)(2,1)}, u32[]{:S(2)}, u32[]{:S(2)}) collective-permute-start(bf16[1024,1024]{1,0:T(8,128)(2,1)} %pad_maximum_fusion), channel_id=1, source_target_pairs={{0,2},{1,3},{2,0},{3,1},{4,6},{5,7},{6,4},{7,5},{8,10},{9,11},{10,... | collective-permute-start | bytes 6291464 | tf_op jit(solution)/shard_map/ppermute | solution.py:136
  161.1 1104.6 %reduce-scatter.15.cloned.1.call-start = ((), (), s32[]{:S(2)}) async-start(), calls=%async_computation.20 | async-start | bytes 5242880 | tf_op jit(solution)/shard_map/reduce_scatter | solution.py:226
  183.8 241.2 %collective-permute-start.3 = (bf16[1024,1024]{1,0:T(8,128)(2,1)}, bf16[1024,1024]{1,0:T(8,128)(2,1)}, u32[]{:S(2)}, u32[]{:S(2)}) collective-permute-start(bf16[1024,1024]{1,0:T(8,128)(2,1)} %pad_maximum_fusion.1), channel_id=1, source_target_pairs={{0,2},{1,3},{2,0},{3,1},{4,6},{5,7},{6,4},{7,5},{8,10},{9,11},{10,... | collective-permute-start | bytes 6291464 | tf_op jit(solution)/shard_map/ppermute | solution.py:136
  1049.0 258.4 %reduce-scatter.11.cloned.1.call-start = ((), (), s32[]{:S(2)}) async-start(), calls=%async_computation.18 | async-start | bytes 5242880 | tf_op jit(solution)/shard_map/reduce_scatter | solution.py:226
  1232.9 154.2 %reduce-scatter.17.cloned.1.call-start = ((), (), s32[]{:S(2)}) async-start(), calls=%async_computation.21 | async-start | bytes 5242880 | tf_op jit(solution)/shard_map/reduce_scatter | solution.py:229
  1233.6 233.0 %reduce-scatter.13.cloned.1.call-start = ((), (), s32[]{:S(2)}) async-start(), calls=%async_computation.19 | async-start | bytes 5242880 | tf_op jit(solution)/shard_map/reduce_scatter | solution.py:229
  1234.2 384.9 %reduce-scatter.19.cloned.1.call-start = ((), (), s32[]{:S(2)}) async-start(), calls=%async_computation.22 | async-start | bytes 4325376 | tf_op jit(solution)/shard_map/reduce_scatter | solution.py:269
  1241.6 528.3 %reduce-scatter.25.cloned.1.call-start = ((), (), s32[]{:S(2)}) async-start(), calls=%async_computation.25 | async-start | bytes 4325376 | tf_op jit(solution)/shard_map/reduce_scatter | solution.py:272
  1248.3 662.9 %all-reduce.3.cloned.1.call-start = ((), (), s32[]{:S(2)}) async-start(), calls=%async_computation.28 | async-start | bytes 181248 | tf_op jit(solution)/shard_map/psum | solution.py:276
  1477.3 587.0 %reduce-scatter.21.cloned.1.call-start = ((), (), s32[]{:S(2)}) async-start(), calls=%async_computation.23 | async-start | bytes 4325376 | tf_op jit(solution)/shard_map/reduce_scatter | solution.py:270
  1483.9 730.7 %reduce-scatter.23.cloned.1.call-start = ((), (), s32[]{:S(2)}) async-start(), calls=%async_computation.24 | async-start | bytes 4325376 | tf_op jit(solution)/shard_map/reduce_scatter | solution.py:271
  1490.3 1086.4 %reduce-scatter.27.cloned.1.call-start = ((), (), s32[]{:S(2)}) async-start(), calls=%async_computation.26 | async-start | bytes 17301504 | tf_op jit(solution)/shard_map/reduce_scatter | solution.py:273
  1516.3 1425.3 %reduce-scatter.29.cloned.1.call-start = ((), (), s32[]{:S(2)}) async-start(), calls=%async_computation.27 | async-start | bytes 17301504 | tf_op jit(solution)/shard_map/reduce_scatter | solution.py:274
  (138 other events, 2938.3 us)
Sparse Core Ops, SparseCore 0:
  10.9 59.0 all-gather.10
  73.0 55.1 all-gather.14
  131.2 253.4 all-gather.8
  386.1 79.5 all-gather.12
  467.1 79.2 all-gather.22
  549.2 54.9 all-gather.16
  607.1 75.9 all-gather.18
  686.0 75.7 all-gather.20
  1049.1 75.4 reduce-scatter.14
  1232.1 75.3 reduce-scatter.10
  1309.8 77.3 reduce-scatter.16
  1389.3 77.2 reduce-scatter.12
  1469.5 149.5 reduce-scatter.18
  1621.8 148.0 reduce-scatter.24
  1777.3 133.8 all-reduce.2
  1913.9 150.3 reduce-scatter.20
  2066.9 147.6 reduce-scatter.22
  2217.3 359.3 reduce-scatter.26
  2579.6 361.9 reduce-scatter.28
